TPU v7x, 256 devices: a whole 4x4x8 slice. The times are simulated.
256 devices in a mesh: section: 4 (over z_lo, core), dp: 64 (over x, y, z_hi).
Axes of the slice: x: 4, y: 4, z: 8 (z_hi: 4, z_lo: 2; z = z_hi * 2 + z_lo), core: 2. Of those that a mesh axis runs over, the one named last changes fastest.
Arguments:
- acts: bfloat16 [4, 24576, 4096], P('section', 'dp'), may hold values from -6 to 6
- cotangent: bfloat16 [24576, 4096], P('dp'), may hold values from -6 to 6
- gains: float32 [4, 4096], P('section'), may hold values from 0.1 to 1.9
- value_w: bfloat16 [4, 4096, 1024], P('section', 'dp'), may hold values from -0.09375 to 0.09375
- output_w: bfloat16 [4, 1024, 4096], P('section', None, 'dp'), may hold values from -0.1875 to 0.1875
- d_map: int32 [4, 64], P('section'), may hold values from 0 to 3
- r_map: int32 [4, 16], P('section'), may hold values from 0 to 3
- lengths: int32 [192], P('dp'), may hold values from 32 to 128, as said below
- item_panels: bfloat16 [64, 4, 2, 128, 128], P('dp', 'section'), may hold values from -24 to 24
- owners: int32 [64], replicated, may hold values from 0 to 63, each once
Outputs:
- grad_in: bfloat16 [4, 24576, 4096], P('section', 'dp')
- scores: float32 [192, 64], P('dp')
Inputs may be any that keep to these rules, and one draw needn't show every extreme that they name: `lengths`: some document is fully live (128 tokens) in every draw.
All inputs are finite; a program needn't handle non-finite values.
Results may differ from a plain program's by a relative error of at most 0.015.
Values may be sent and summed in bfloat16 or wider, within the bound.
No kernel may reach another device: no remote copies, remote signals or barrier semaphores. Data moves between devices by JAX's collectives and lax.ppermute only.
A program may use at most 128 MiB of HBM per device.

v0:
```python
import jax
import jax.numpy as jnp
from jax import lax
from jax.sharding import PartitionSpec as P

BLOCK = 64
DBINS = 2
RBINS = 2


def shifted(block, axis, distance):
    devices = range(lax.axis_size(axis))
    route = [(i - distance, i) for i in devices if i - distance in devices]
    return lax.ppermute(block, axis, route)


def normalize(inputs, gain_row):
    return inputs * lax.rsqrt(jnp.mean(inputs * inputs, axis=-1, keepdims=True) + 1e-05) * gain_row


def sketch_matrix(codes, bin_count):
    levels = jnp.arange(bin_count, dtype=jnp.int32)
    sign_row = (1 - 2 * (codes // bin_count)).astype(jnp.bfloat16)
    return jnp.where(
        levels[:, None] == (codes % bin_count)[None, :],
        sign_row[None, :],
        jnp.zeros_like(sign_row)[None, :],
    )


def project_rows(values, sketch):
    row_count = values.shape[0]
    block_count = values.shape[1] // BLOCK
    bin_count = sketch.shape[0]
    pieces = values.reshape(row_count, block_count, BLOCK)
    mapped = jnp.einsum("tbc,kb->tkc", pieces, sketch, preferred_element_type=jnp.float32)
    return mapped.reshape(row_count, bin_count * BLOCK) * (block_count / bin_count) ** (-0.5)


def section_work(
    inputs_bf, current, gain_row, value_full, output_full, model_sketch, value_sketch, doc_lens
):
    row_count = inputs_bf.shape[0]
    doc_count = doc_lens.shape[0]
    slot_count = row_count // doc_count
    inputs = inputs_bf.astype(jnp.float32)
    hidden = normalize(inputs, gain_row).astype(jnp.bfloat16)
    values = jnp.dot(hidden, value_full, preferred_element_type=jnp.float32).astype(jnp.bfloat16)
    dvalues = lax.dot_general(
        current, output_full, (((1,), (1,)), ((), ())), preferred_element_type=jnp.float32
    ).astype(jnp.bfloat16)
    dhidden = lax.dot_general(
        dvalues, value_full, (((1,), (1,)), ((), ())), preferred_element_type=jnp.float32
    )
    _, pullback = jax.vjp(lambda probe: normalize(probe, gain_row), inputs)
    grad_next = (current.astype(jnp.float32) + pullback(dhidden)[0]).astype(jnp.bfloat16)
    hidden_proj = project_rows(hidden, model_sketch).reshape(doc_count, slot_count, -1)
    dvalue_proj = project_rows(dvalues, value_sketch).reshape(doc_count, slot_count, -1)
    grad_proj = project_rows(current, model_sketch).reshape(doc_count, slot_count, -1)
    value_proj = project_rows(values, value_sketch).reshape(doc_count, slot_count, -1)
    first_feat = jnp.einsum(
        "dtk,dtj->dkj", hidden_proj, dvalue_proj, precision=lax.Precision.HIGHEST
    )
    second_feat = jnp.einsum("dtk,dtj->dkj", grad_proj, value_proj, precision=lax.Precision.HIGHEST)
    inverse_len = 1.0 / doc_lens.astype(jnp.float32)
    features = jnp.stack([first_feat, second_feat], axis=1) * inverse_len[:, None, None, None]
    return (grad_next, features.reshape(doc_count, -1))


def body(acts, cotangent, gains, value_w, output_w, d_map, r_map, lengths, item_panels, owners):
    section_count = lax.axis_size("section")
    section_id = lax.axis_index("section")
    last_section = section_count - 1
    value_full, output_full = (
        lax.all_gather(value_w[0], "dp", axis=0, tiled=True),
        lax.all_gather(output_w[0], "dp", axis=1, tiled=True),
    )
    model_sketch = sketch_matrix(d_map[0], DBINS)
    value_sketch = sketch_matrix(r_map[0], RBINS)
    gain_row = gains[0]
    layer_inputs = acts[0]
    token_count = layer_inputs.shape[0]
    model_width = layer_inputs.shape[1]
    doc_count = lengths.shape[0]
    slot_count = token_count // doc_count
    feature_width = item_panels.shape[2] * item_panels.shape[3] * item_panels.shape[4]
    group_count = 1
    group_rows = token_count // group_count
    positions = jnp.arange(slot_count, dtype=jnp.int32)

    def advance(turn, carry):
        incoming, grad_store, feat_store = carry
        group_id = turn - (last_section - section_id)
        is_live = (group_id >= 0) & (group_id < group_count)
        cot_rows = cotangent
        live_mask = (positions[None, :] < lengths[:, None]).reshape(group_rows, 1)
        cot_rows = jnp.where(live_mask, cot_rows, jnp.zeros_like(cot_rows))
        current = jnp.where(section_id == last_section, cot_rows, incoming)

        def active(stores):
            grad_next, features = section_work(
                layer_inputs,
                current,
                gain_row,
                value_full,
                output_full,
                model_sketch,
                value_sketch,
                lengths,
            )
            return (grad_next, grad_next, features)

        def resting(stores):
            return (jnp.zeros_like(incoming), stores[0], stores[1])

        outgoing, grad_store, feat_store = lax.cond(
            is_live, active, resting, (grad_store, feat_store)
        )
        incoming = shifted(outgoing, "section", -1)
        return (incoming, grad_store, feat_store)

    start_state = (
        jnp.zeros((group_rows, model_width), jnp.bfloat16),
        jnp.zeros((token_count, model_width), jnp.bfloat16),
        jnp.zeros((doc_count, feature_width), jnp.float32),
    )
    _, grad_store, feat_store = lax.fori_loop(
        0, section_count + group_count - 1, advance, start_state
    )
    features = feat_store.astype(jnp.bfloat16)
    own_panels = item_panels[:, 0].reshape(item_panels.shape[0], feature_width)
    per_owner = own_panels.shape[0]
    owner_count = lax.axis_size("dp")
    all_rows = lax.all_gather(own_panels, "dp", axis=0, tiled=True)
    products = lax.dot_general(
        features, all_rows, (((1,), (1,)), ((), ())), preferred_element_type=jnp.float32
    )
    collected = jnp.take(
        products.reshape(doc_count, owner_count, per_owner), owners, axis=1
    ).reshape(doc_count, owner_count * per_owner)
    scaled = collected * (feature_width // 2) ** (-0.5)
    scores = lax.psum(scaled, "section")
    return (grad_store[None], scores)


def solution(mesh):
    in_specs = (
        P("section", "dp", None),
        P("dp", None),
        P("section", None),
        P("section", "dp", None),
        P("section", None, "dp"),
        P("section", None),
        P("section", None),
        P("dp"),
        P("dp", "section", None, None, None),
        P(),
    )
    out_specs = (P("section", "dp", None), P("dp", None))
    return jax.shard_map(body, mesh=mesh, in_specs=in_specs, out_specs=out_specs, check_vma=False)
```

profile of v0, /device:TPU:1, one launch (start us, length us, event | category | flops | bytes accessed | tf_op | source)
XLA Modules:
  0.0 736.3 jit_solution(3170895180347043980)
XLA Ops:
  15.2 107.8 %all-gather.7.cloned.1.call-done = bf16[1,1024,4096]{1,2,0:T(8,128)(2,1)} async-done(((bf16[1,1024,64]{1,2,0:T(8,128)(2,1)}), bf16[1,1024,4096]{1,2,0:T(8,128)(2,1)}) %all-gather.7.cloned.1.call-update) | async-done | bytes 8388624 | tf_op jit(solution)/shard_map/all_gather | solution.py:76
  123.0 11.4 %copy.56 = bf16[1024,4096]{1,0:T(8,128)(2,1)} copy(bf16[1024,4096]{0,1:T(8,128)(2,1)} %bitcast.69) | data formatting | bytes 16777216
  134.4 105.7 %all-gather.11.cloned.1.call-done = bf16[64,1,32768]{2,1,0:T(2,128)(2,1)} async-done(((bf16[1,1,32768]{2,1,0:T(2,128)(2,1)}), bf16[64,1,32768]{2,1,0:T(2,128)(2,1)}) %all-gather.11.cloned.1.call-update) | async-done | bytes 4194320 | tf_op jit(solution)/shard_map/all_gather | solution.py:134
  240.0 116.5 %all-gather.9.cloned.1.call-done = bf16[1,4096,1024]{2,1,0:T(8,128)(2,1)} async-done(((bf16[1,64,1024]{2,1,0:T(8,128)(2,1)}), bf16[1,4096,1024]{2,1,0:T(8,128)(2,1)}) %all-gather.9.cloned.1.call-update) | async-done | bytes 8388624 | tf_op jit(solution)/shard_map/all_gather | solution.py:75
  361.4 348.6 %while.20 = (s32[]{:T(128)}, bf16[384,4096]{1,0:T(8,128)(2,1)}, bf16[384,4096]{1,0:T(8,128)(2,1)}, bf16[3,32768]{1,0:T(4,128)(2,1)}, s32[]{:T(128)}, /*index=5*/...) while((s32[]{:T(128)}, bf16[384,4096]{1,0:T(8,128)(2,1)}, ...), condition=%wide.region_5.6_spmd.clone, body=%wide.region_0.5_spmd.clone.sunk | while | flops 9861564416 | bytes 184798928 | solution.py:127
  363.6 2.6 collective-permute-start
  366.1 42.7 %collective-permute-done = bf16[384,4096]{1,0:T(8,128)(2,1)S(1)} collective-permute-done((bf16[384,4096]{1,0:T(8,128)(2,1)}, bf16[384,4096]{1,0:T(8,128)(2,1)S(1)}, u32[]{:S(2)}, u32[]{:S(2)}) %collective-permute-start) | collective-permute-done | bytes 3145760 | tf_op jit(solution)/shard_map/while/body/eval_jaxpr/ppermute | solution.py:14
  414.6 137.4 %collective-permute-done = bf16[384,4096]{1,0:T(8,128)(2,1)S(1)} collective-permute-done((bf16[384,4096]{1,0:T(8,128)(2,1)}, bf16[384,4096]{1,0:T(8,128)(2,1)S(1)}, u32[]{:S(2)}, u32[]{:S(2)}) %collective-permute-start) | collective-permute-done | bytes 3145760 | tf_op jit(solution)/shard_map/while/body/eval_jaxpr/ppermute | solution.py:14
  553.7 68.8 %conditional.3 = (bf16[384,4096]{1,0:T(8,128)(2,1)}, bf16[384,4096]{1,0:T(8,128)(2,1)}, bf16[3,32768]{1,0:T(4,128)(2,1)}) conditional(s32[]{:T(128)} %convert_element_type.77, (bf16[384,4096]{1,0:T(8,128)(2,1)}, bf16[3,32768]{1,0:T(4,128)(2,1)}) %tuple.73, (pred[]{:T(512)}, s32[128]{0:T(128)S(1)}, s32[3]{0:T(128)}, bf16[384,4096]{1,0:T(8,128)(2,1)}, ...), branch_computations={%region_1.1_spmd, %region_2.4_spmd} | conditional | flops 9861564416 | bytes 159631488 | solution.py:116
  554.5 3.4 select_select_fusion
  559.7 3.4 convolution_convert_fusion.1
  563.2 6.6 fusion.8
  569.8 4.3 fusion.11
  574.1 4.7 copy.39
  580.0 3.7 fusion.27
  594.4 8.7 %convolution_convert_fusion = bf16[384,1024]{1,0:T(8,128)(2,1)} fusion(bf16[384,4096]{1,0:T(8,128)(2,1)} %get-tuple-element.529, bf16[4096,1024]{1,0:T(8,128)(2,1)} %get-tuple-element.384), kind=kOutput, calls=%fused_computation.21 | convolution fusion | flops 3221618688 | bytes 12320768 | tf_op jit(solution)/shard_map/while/body/eval_jaxpr/cond/branch_1_fun/dot_general | solution.py:48
  609.9 2.9 copy.47
  612.7 3.8 fusion.24
  618.7 3.9 copy.95
  624.5 36.9 %collective-permute-done = bf16[384,4096]{1,0:T(8,128)(2,1)S(1)} collective-permute-done((bf16[384,4096]{1,0:T(8,128)(2,1)}, bf16[384,4096]{1,0:T(8,128)(2,1)S(1)}, u32[]{:S(2)}, u32[]{:S(2)}) %collective-permute-start) | collective-permute-done | bytes 3145760 | tf_op jit(solution)/shard_map/while/body/eval_jaxpr/ppermute | solution.py:14
  665.2 37.6 %collective-permute-start = (bf16[384,4096]{1,0:T(8,128)(2,1)}, bf16[384,4096]{1,0:T(8,128)(2,1)S(1)}, u32[]{:S(2)}, u32[]{:S(2)}) collective-permute-start(bf16[384,4096]{1,0:T(8,128)(2,1)} %get-tuple-element.638), channel_id=1, source_target_pairs={{64,0},{128,64},{192,128},{65,1},{129,65},{193,129},{66,2},{130,66... | collective-permute-start | bytes 9437192 | tf_op jit(solution)/shard_map/while/body/eval_jaxpr/ppermute | solution.py:14
  702.8 5.5 collective-permute-done
  710.0 8.0 %fusion.37 = f32[3,64]{0,1:T(8,128)S(1)} fusion(bf16[64,1,32768]{2,1,0:T(2,128)(2,1)} %all-gather.11.cloned.1.call-done, bf16[3,32768]{1,0:T(4,128)(2,1)} %get-tuple-element.413), kind=kOutput, calls=%fused_computation.48 | convolution fusion | flops 12582912 | bytes 4391680 | tf_op jit(solution)/shard_map/dot_general | solution.py:135
  718.8 10.3 %psum.7 = f32[3,64]{0,1:T(8,128)S(1)} all-reduce(f32[3,64]{0,1:T(8,128)S(1)} %multiply_bitcast_fusion), channel_id=1, replica_groups=mesh['section'=4,'dp'=64] {'section'}, use_global_device_ids=true, to_apply=%region_6.7 | all-reduce | flops 192 | bytes 1536 | tf_op jit(solution)/shard_map/psum | solution.py:142
  (90 shorter events, 61.2 us)
Async XLA Ops:
  7.2 115.8 %all-gather.7.cloned.1.call-start = ((), (), s32[]{:S(2)}) async-start(), calls=%async_computation | async-start | bytes 8519680 | tf_op jit(solution)/shard_map/all_gather | solution.py:76
  7.9 232.1 %all-gather.11.cloned.1.call-start = ((), (), s32[]{:S(2)}) async-start(), calls=%async_computation.2 | async-start | bytes 8519680 | tf_op jit(solution)/shard_map/all_gather | solution.py:134
  9.5 347.0 %all-gather.9.cloned.1.call-start = ((), (), s32[]{:S(2)}) async-start(), calls=%async_computation.1 | async-start | bytes 8519680 | tf_op jit(solution)/shard_map/all_gather | solution.py:75
  356.5 4.9 copy-start.6
  363.6 45.3 %collective-permute-start = (bf16[384,4096]{1,0:T(8,128)(2,1)}, bf16[384,4096]{1,0:T(8,128)(2,1)S(1)}, u32[]{:S(2)}, u32[]{:S(2)}) collective-permute-start(bf16[384,4096]{1,0:T(8,128)(2,1)} %get-tuple-element.638), channel_id=1, source_target_pairs={{64,0},{128,64},{192,128},{65,1},{129,65},{193,129},{66,2},{130,66... | collective-permute-start | bytes 9437192 | tf_op jit(solution)/shard_map/while/body/eval_jaxpr/ppermute | solution.py:14
  408.9 1.7 copy-start
  412.7 139.3 %collective-permute-start = (bf16[384,4096]{1,0:T(8,128)(2,1)}, bf16[384,4096]{1,0:T(8,128)(2,1)S(1)}, u32[]{:S(2)}, u32[]{:S(2)}) collective-permute-start(bf16[384,4096]{1,0:T(8,128)(2,1)} %get-tuple-element.638), channel_id=1, source_target_pairs={{64,0},{128,64},{192,128},{65,1},{129,65},{193,129},{66,2},{130,66... | collective-permute-start | bytes 9437192 | tf_op jit(solution)/shard_map/while/body/eval_jaxpr/ppermute | solution.py:14
  552.0 1.7 copy-start
  554.5 5.2 copy-start.5
  559.7 3.5 copy-start.1
  563.1 6.6 copy-start.2
  579.5 0.5 copy-start.7
  587.5 0.5 copy-start.9
  594.4 11.0 %copy-start.10 = (bf16[2,16,1]{1,0,2:T(2,128)(2,1)S(1)}, bf16[2,16,1]{1,0,2:T(2,128)(2,1)}, u32[]{:S(2)}) copy-start(bf16[2,16,1]{1,0,2:T(2,128)(2,1)} %copy-done.9) | copy-start | bytes 196 | tf_op jit(solution)/shard_map/while/body/eval_jaxpr/cond
  609.8 2.9 copy-start.8
  612.7 3.9 copy-start.4
  612.7 4.2 copy-start.3
  622.6 38.8 %collective-permute-start = (bf16[384,4096]{1,0:T(8,128)(2,1)}, bf16[384,4096]{1,0:T(8,128)(2,1)S(1)}, u32[]{:S(2)}, u32[]{:S(2)}) collective-permute-start(bf16[384,4096]{1,0:T(8,128)(2,1)} %get-tuple-element.638), channel_id=1, source_target_pairs={{64,0},{128,64},{192,128},{65,1},{129,65},{193,129},{66,2},{130,66... | collective-permute-start | bytes 9437192 | tf_op jit(solution)/shard_map/while/body/eval_jaxpr/ppermute | solution.py:14
  661.4 1.7 copy-start
  665.2 43.1 %collective-permute-start = (bf16[384,4096]{1,0:T(8,128)(2,1)}, bf16[384,4096]{1,0:T(8,128)(2,1)S(1)}, u32[]{:S(2)}, u32[]{:S(2)}) collective-permute-start(bf16[384,4096]{1,0:T(8,128)(2,1)} %get-tuple-element.638), channel_id=1, source_target_pairs={{64,0},{128,64},{192,128},{65,1},{129,65},{193,129},{66,2},{130,66... | collective-permute-start | bytes 9437192 | tf_op jit(solution)/shard_map/while/body/eval_jaxpr/ppermute | solution.py:14
  708.3 1.7 copy-start
  710.0 8.7 %copy-start.11 = (pred[64]{0:T(512)(128)(4,1)S(1)}, pred[64]{0:T(512)(128)(4,1)}, u32[]{:S(2)}) copy-start(pred[64]{0:T(512)(128)(4,1)} %compare_and_fusion) | copy-start | bytes 196
Sparse Core Ops, SparseCore 0:
  11.3 111.6 all-gather.6
  126.9 113.1 all-gather.10
  243.3 113.1 all-gather.8
where the time goes:
time: 737 us; the launch traced here: 736 us
  waiting for transfers between devices  554 us (75%)
  local copies, waits for them, and re-layouts  56.6 us (8%)
  starting transfers between devices  44.1 us (6%)
  matrix products  41.1 us (6%)
  other arithmetic  16.5 us (2%)
  between operations  13.8 us (2%)
  blocking collectives  10.3 us (1%)
    ppermute x4, waiting for transfers between devices, shifted(): return lax.ppermute(block, axis, route)  222 us
    all_gather x1, waiting for transfers between devices, body(): lax.all_gather(value_w[0], 'dp', axis=0, tiled=True)  116 us
    all_gather x1, waiting for transfers between devices, body(): lax.all_gather(output_w[0], 'dp', axis=1, tiled=True)  108 us
    all_gather x1, waiting for transfers between devices, body(): all_rows = lax.all_gather(own_panels, 'dp', axis=0, tiled=True)  106 us
    ppermute x4, starting transfers between devices, shifted(): return lax.ppermute(block, axis, route)  44 us
  transfers between devices with their start and end apart: 7, of which 7 were waited for; matrix products, arithmetic and copies ran while one was open for 2% of the time, Pallas kernels for 0%

commit v1 on v0

v1 whole, which is shorter than its diff:
```python
import functools

import jax
import jax.numpy as jnp
from jax import lax
from jax.experimental import pallas as pl
from jax.experimental.pallas import tpu as pltpu
from jax.sharding import PartitionSpec as P

BLOCK = 64
EPS = 1e-05
ANY = pl.BlockSpec(memory_space=pl.ANY)
SMEM = pl.BlockSpec(memory_space=pltpu.SMEM)
VMEM = pl.BlockSpec(memory_space=pltpu.VMEM)
F32 = jnp.float32
BF16 = jnp.bfloat16
TILES = 8


def projection(codes, width):
    row = lax.broadcasted_iota(jnp.int32, (width, 2 * BLOCK), 0)
    col = lax.broadcasted_iota(jnp.int32, (width, 2 * BLOCK), 1)
    code = jnp.broadcast_to(codes[:, None, None], (codes.shape[0], BLOCK, 2 * BLOCK))
    code = code.reshape(width, 2 * BLOCK)
    hit = (row % BLOCK == col % BLOCK) & (code % 2 == col // BLOCK)
    return jnp.where(hit, 1 - 2 * (code // 2), 0).astype(BF16)


def chain_kernel(
    stage, chunk, rows, meta, g_hbm, x_hbm, gain, w_hbm, pm_hbm, qm, grads_in, gp_in, dvp_in,
    send, grads, gp, dvp,
    wo_s, wv_s, g_s, x_s, pm_s, u_s, out_s, acc_s, dv_s, p_s, w_sem, in_sem, out_sem,
):
    shards, depth = wo_s.shape[0], wo_s.shape[2]
    width = shards * wo_s.shape[1]
    per = shards // TILES
    step = width // TILES
    base = chunk * rows

    def weight(kind, dst, t):
        at = pl.ds(pl.multiple_of(t * per, per), per)
        return pltpu.make_async_copy(w_hbm.at[at, kind], dst.at[at], w_sem.at[1 - kind, t])

    def columns(t):
        return pl.ds(pl.multiple_of(t * step, step), step)

    def result(t, i):
        at = columns(t)
        dst = grads.at[pl.ds(base, rows), at] if i == 0 else send.at[:, at]
        return pltpu.make_async_copy(out_s.at[:, at], dst, out_sem.at[i, t])

    def small(i):
        dst = (gp, dvp)[i].at[pl.ds(base, rows)]
        return pltpu.make_async_copy(p_s.at[i], dst, in_sem.at[3 + i])

    results = range(1 if send is None else 2)

    @pl.when(meta[0] == stage)
    def _():
        cg = pltpu.make_async_copy(g_hbm, g_s, in_sem.at[0])
        cx = pltpu.make_async_copy(x_hbm.at[pl.ds(base, rows)], x_s, in_sem.at[1])
        cp = pltpu.make_async_copy(pm_hbm, pm_s, in_sem.at[2])
        cg.start()
        weight(1, wo_s, 0).start()
        cx.start()

        def begin(kind, dst, first):
            @pl.loop(first, TILES)
            def _(t):
                weight(kind, dst, t).start()

        begin(1, wo_s, 1)
        begin(0, wv_s, 0)
        cp.start()
        acc_s[...] = jnp.zeros_like(acc_s)
        cg.wait()

        @pl.loop(0, TILES)
        def _(t):
            weight(1, wo_s, t).wait()
            acc_s[...] += jnp.dot(
                g_s[:, columns(t)],
                wo_s[pl.ds(pl.multiple_of(t * per, per), per)].reshape(step, depth),
                preferred_element_type=F32,
            )

        dv_s[...] = acc_s[...].astype(BF16)
        cx.wait()

        def back(t, sums):
            weight(0, wv_s, t).wait()
            dh = lax.dot_general(
                dv_s[...],
                wv_s[pl.ds(pl.multiple_of(t * per, per), per)].reshape(step, depth),
                (((1,), (1,)), ((), ())),
                preferred_element_type=F32,
            )
            at = columns(t)
            u = dh * gain[:, at]
            x = x_s[:, at].astype(F32)
            u_s[:, at] = u
            return (
                sums[0] + jnp.sum(u * x, axis=-1, keepdims=True),
                sums[1] + jnp.sum(x * x, axis=-1, keepdims=True),
            )

        zero = jnp.zeros((rows, 1), F32)
        total, square = lax.fori_loop(0, TILES, back, (zero, zero))
        r = lax.rsqrt(square * (1.0 / width) + EPS)
        drop = r * r * r * total * (1.0 / width)

        @pl.loop(0, TILES)
        def _(t):
            at = columns(t)
            grad = g_s[:, at].astype(F32) + (r * u_s[:, at] - drop * x_s[:, at].astype(F32))
            out_s[:, at] = grad.astype(BF16)
            for i in results:
                result(t, i).start()

        cp.wait()
        p_s[0] = jnp.dot(g_s[...], pm_s[...], preferred_element_type=F32)
        p_s[1] = jnp.dot(dv_s[...], qm[...], preferred_element_type=F32)
        for i in range(2):
            small(i).start()

        @pl.loop(0, TILES)
        def _(t):
            for i in results:
                result(t, i).wait()

        for i in range(2):
            small(i).wait()


def chain(stage, chunk, meta, g, x, gain, w, pm, qm, state):
    rows, width = g.shape
    shards, _, per_shard, depth = w.shape
    last = stage == 0
    kernel = functools.partial(chain_kernel, stage, chunk, rows)
    if last:
        def kernel(*refs):
            return chain_kernel(stage, chunk, rows, *refs[:10], None, *refs[10:])
    out_shape = [jax.ShapeDtypeStruct(s.shape, s.dtype) for s in state]
    if not last:
        out_shape = [jax.ShapeDtypeStruct((rows, width), BF16)] + out_shape
    off = 0 if last else 1
    outs = pl.pallas_call(
        kernel,
        out_shape=out_shape,
        in_specs=[SMEM, ANY, ANY, VMEM, ANY, ANY, VMEM, ANY, ANY, ANY],
        out_specs=[ANY] * len(out_shape),
        input_output_aliases={7: off, 8: off + 1, 9: off + 2},
        scratch_shapes=[
            pltpu.VMEM((shards, per_shard, depth), BF16),
            pltpu.VMEM((shards, per_shard, depth), BF16),
            pltpu.VMEM((rows, width), BF16),
            pltpu.VMEM((rows, width), BF16),
            pltpu.VMEM(pm.shape, BF16),
            pltpu.VMEM((rows, width), F32),
            pltpu.VMEM((rows, width), BF16),
            pltpu.VMEM((rows, depth), F32),
            pltpu.VMEM((rows, depth), BF16),
            pltpu.VMEM((2, rows, 2 * BLOCK), F32),
            pltpu.SemaphoreType.DMA((2, TILES)),
            pltpu.SemaphoreType.DMA((5,)),
            pltpu.SemaphoreType.DMA((2, TILES)),
        ],
        compiler_params=pltpu.CompilerParams(vmem_limit_bytes=44 << 20),
        cost_estimate=pl.CostEstimate(
            flops=4 * rows * width * depth, bytes_accessed=4 * width * depth, transcendentals=0
        ),
        name=f"chain_{stage}_{chunk}",
    )(meta, g, x, gain, w, pm, qm, *state)
    if last:
        return None, tuple(outs)
    return outs[0], tuple(outs[1:])


def value_kernel(h, w_hbm, qm, after, out, wv_s, acc_s, w_sem):
    shards, depth = wv_s.shape[0], wv_s.shape[2]
    per = shards // TILES
    step = shards * wv_s.shape[1] // TILES

    def weight(t):
        at = pl.ds(pl.multiple_of(t * per, per), per)
        return pltpu.make_async_copy(w_hbm.at[at, 0], wv_s.at[at], w_sem.at[t])

    @pl.loop(0, TILES)
    def _(t):
        weight(t).start()

    acc_s[...] = jnp.zeros_like(acc_s)

    @pl.loop(0, TILES)
    def _(t):
        weight(t).wait()
        acc_s[...] += jnp.dot(
            h[:, pl.ds(pl.multiple_of(t * step, step), step)],
            wv_s[pl.ds(pl.multiple_of(t * per, per), per)].reshape(step, depth),
            preferred_element_type=F32,
        )

    out[...] = jnp.dot(acc_s[...].astype(BF16), qm[...], preferred_element_type=F32)


def value_proj(h, w, qm, after):
    shards, _, per_shard, depth = w.shape
    rows, width = h.shape
    return pl.pallas_call(
        value_kernel,
        out_shape=jax.ShapeDtypeStruct((rows, 2 * BLOCK), F32),
        in_specs=[VMEM, ANY, VMEM, ANY],
        out_specs=VMEM,
        scratch_shapes=[
            pltpu.VMEM((shards, per_shard, depth), BF16),
            pltpu.VMEM((rows, depth), F32),
            pltpu.SemaphoreType.DMA((TILES,)),
        ],
        compiler_params=pltpu.CompilerParams(vmem_limit_bytes=40 << 20),
        cost_estimate=pl.CostEstimate(
            flops=2 * rows * width * depth, bytes_accessed=2 * width * depth, transcendentals=0
        ),
        name="value_proj",
    )(h, w, qm, after)


def score_kernel(docs, scale, owners, lens, hp, vp, gp, dvp, panels, out, feat_s, acc_s):
    slots = hp.shape[0] // docs
    side = hp.shape[1]
    dims = (((0,), (0,)), ((), ()))
    for d in range(docs):
        rows = slice(d * slots, (d + 1) * slots)
        inv = scale / lens[d].astype(F32)
        for i, (a, b) in enumerate(((hp, dvp), (gp, vp))):
            f = lax.dot_general(
                a[rows, :], b[rows, :], dims, precision=lax.Precision.HIGHEST,
                preferred_element_type=F32,
            )
            feat_s[d, i * side : (i + 1) * side, :] = (f * inv).astype(BF16).astype(F32)

    def item(j, carry):
        p = panels[owners[j]].astype(F32)
        for d in range(docs):
            acc_s[d, pl.ds(j, 1), :] = jnp.sum(p * feat_s[d], axis=0, keepdims=True)
        return carry

    lax.fori_loop(0, panels.shape[0], item, 0)
    ones = jnp.ones((8, side), F32)
    for d in range(docs):
        total = lax.dot_general(
            ones, acc_s[d], (((1,), (1,)), ((), ())), precision=lax.Precision.HIGHEST,
            preferred_element_type=F32,
        )
        out[d : d + 1, :] = total[:1] * (1.0 / side)


def score(owners, lens, hp, vp, gp, dvp, panels):
    docs = lens.shape[0]
    items, high, side = panels.shape
    return pl.pallas_call(
        functools.partial(score_kernel, docs, 1.0 / 16),
        out_shape=jax.ShapeDtypeStruct((docs, items), F32),
        in_specs=[SMEM, SMEM] + [VMEM] * 5,
        out_specs=VMEM,
        scratch_shapes=[
            pltpu.VMEM((docs, high, side), F32),
            pltpu.VMEM((docs, items, side), F32),
        ],
        compiler_params=pltpu.CompilerParams(vmem_limit_bytes=32 << 20),
        name="score",
    )(owners, lens, hp, vp, gp, dvp, panels)


def gather_weights(wv, wo):
    w = jnp.stack([wv, wo])[None]
    return lax.all_gather(w, "dp", axis=0, tiled=True)


def body(acts, cotangent, gains, value_w, output_w, d_map, r_map, lengths, item_panels, owners):
    sections = lax.axis_size("section")
    section = lax.axis_index("section")
    x = acts[0]
    tokens, width = x.shape
    docs = lengths.shape[0]
    slots = tokens // docs
    w = gather_weights(value_w[0], output_w[0].T)
    panels = lax.all_gather(item_panels.reshape(1, -1, 2 * BLOCK), "dp", axis=0, tiled=True)

    pm = projection(d_map[0], width)
    qm = projection(r_map[0], value_w.shape[2])
    gain = gains
    xf = x.astype(F32)
    hidden = (xf * lax.rsqrt(jnp.mean(xf * xf, axis=-1, keepdims=True) + EPS) * gain).astype(BF16)
    hp = jnp.dot(hidden, pm, preferred_element_type=F32)
    live = (jnp.arange(slots, dtype=jnp.int32)[None, :] < lengths[:, None]).reshape(docs, slots, 1)
    cot = jnp.where(live, cotangent.reshape(docs, slots, width), 0).astype(BF16)
    meta = section.reshape(1)
    state = (
        jnp.zeros((tokens, width), BF16),
        jnp.zeros((tokens, 2 * BLOCK), F32),
        jnp.zeros((tokens, 2 * BLOCK), F32),
    )
    incoming = [cot[d] for d in range(docs)]
    vp = None
    for stage in range(sections - 1, -1, -1):
        arrived = []
        for d in range(docs):
            send, state = chain(stage, d, meta, incoming[d], x, gain, w, pm, qm, state)
            if stage > 0:
                arrived.append(lax.ppermute(send, "section", [(stage, stage - 1)]))
        incoming = arrived
        if vp is None:
            vp = value_proj(hidden, w, qm, send)
    grads, gp, dvp = state
    part = score(owners, lengths, hp, vp, gp, dvp, panels)
    total = part
    for k in range(1, sections):
        total = total + lax.ppermute(
            part, "section", [(i, (i + k) % sections) for i in range(sections)]
        )
    return (grads[None], total)


def solution(mesh):
    in_specs = (
        P("section", "dp", None),
        P("dp", None),
        P("section", None),
        P("section", "dp", None),
        P("section", None, "dp"),
        P("section", None),
        P("section", None),
        P("dp"),
        P("dp", "section", None, None, None),
        P(),
    )
    out_specs = (P("section", "dp", None), P("dp", None))
    return jax.shard_map(body, mesh=mesh, in_specs=in_specs, out_specs=out_specs, check_vma=False)
```

time: 737 us -> 328 us (0.45)
  waiting for transfers between devices: 554 us -> 200 us
  Pallas kernels: 0 us -> 45.8 us
  matrix products: 41.1 us -> 1.71 us
  local copies, waits for them, and re-layouts: 56.6 us -> 18.2 us
  starting transfers between devices: 44.1 us -> 15.3 us
  other arithmetic: 16.5 us -> 31.6 us
  blocking collectives: 10.3 us -> 0 us
    all_gather x3 -> x2, waiting for transfers between devices: 330 us -> 139 us  [the longest x1 139 us: gather_weights(): return lax.all_gather(w, 'dp', axis=0, tiled=True)]
    ppermute x4 -> x12, waiting for transfers between devices: 222 us -> 60.5 us  [the longest x9 59 us: body(): arrived.append(lax.ppermute(send, 'section', [(stage, stage - 1)]))]
    pallas_call x0 -> x14, Pallas kernels: none -> 45.8 us  [the longest x12 34.5 us: chain(): pl.pallas_call(kernel, out_shape=out_shape, in_specs=[SMEM, ANY, ANY, VME...]
    dot_general x10 -> x1, matrix products: 41.1 us -> 1.71 us  [body(): hp = jnp.dot(hidden, pm, preferred_element_type=F32)]
    ppermute x4 -> x12, starting transfers between devices: 44 us -> 15.2 us  [the longest x9 10.3 us: body(): arrived.append(lax.ppermute(send, 'section', [(stage, stage - 1)]))]
    another operation x6 -> x2, local copies, waits for them, and re-layouts: 10.5 us -> 0.03 us
    psum x1 -> x0, blocking collectives: 10.3 us -> none  [body(): scores = lax.psum(scaled, 'section')]
    convert_element_type x3 -> x0, local copies, waits for them, and re-layouts: 9.4 us -> none  [the longest x1 4.71 us: section_work(): hidden = normalize(inputs, gain_row).astype(jnp.bfloat16)]
  transfers between devices with their start and end apart: 7 -> 14, of which waited for: 7 -> 5; matrix products, arithmetic and copies ran while one was open for 2% -> 12% of each run, Pallas kernels for 0% -> 12%
where the time goes in v1:
time: 328 us; the launch traced here: 327 us
  waiting for transfers between devices  200 us (61%)
  Pallas kernels  45.8 us (14%)
  other arithmetic  31.6 us (10%)
  local copies, waits for them, and re-layouts  18.2 us (6%)
  starting transfers between devices  15.3 us (5%)
  between operations  14.5 us (4%)
    all_gather x1, waiting for transfers between devices, gather_weights(): return lax.all_gather(w, 'dp', axis=0, tiled=True)  139 us
    ppermute x9, waiting for transfers between devices, body(): arrived.append(lax.ppermute(send, 'section', [(stage, stage - 1)]))  59 us
    pallas_call x12, Pallas kernels, chain(): pl.pallas_call(kernel, out_shape=out_shape, in_specs=[SMEM, ANY, ANY, VME...  34.5 us
    convert_element_type x2, other arithmetic, projection(): return jnp.where(hit, 1 - 2 * (code // 2), 0).astype(BF16)  11.1 us
    unnamed x54, local copies, waits for them, and re-layouts  10.6 us
    ppermute x9, starting transfers between devices, body(): arrived.append(lax.ppermute(send, 'section', [(stage, stage - 1)]))  10.3 us
  transfers between devices with their start and end apart: 14, of which 5 were waited for; matrix products, arithmetic and copies ran while one was open for 12% of the time, Pallas kernels for 12%

profile of v1, /device:TPU:1, one launch (start us, length us, event | category | flops | bytes accessed | tf_op | source)
XLA Modules:
  0.0 327.5 jit_solution(1198065123990364355)
XLA Ops:
  7.2 1.7 pad_maximum_fusion
  18.7 2.7 fusion
  24.1 2.8 fusion.47.qm.refs_6_
  27.0 8.3 %fusion.12.pm_hbm.refs_5_ = bf16[4096,128]{1,0:T(8,128)(2,1)} fusion(s32[4096]{0:T(1024)S(1)} %broadcast_in_dim.115, s32[4096]{0:T(1024)} %get-tuple-element.102, s32[128]{0:T(128)} %get-tuple-element.117, s32[128]{0:T(128)} %get-tuple-element.119, s32[4096]{0:T(1024)} %get-tuple-element.101, s32[4096]{0:T(1024)} %get-tuple-element.100, ...), kind=kLoop, calls=%fused_computation.29 | loop fusion | flops 11534336 | bytes 1165568 | tf_op jit(solution)/shard_map/convert_element_type | solution.py:26
  35.6 1.7 slice_bitcast_fusion
  37.3 139.2 %all-gather.6.cloned.1.call-done = bf16[128,64,1024]{2,1,0:T(8,128)(2,1)} async-done(((bf16[2,64,1024]{2,1,0:T(8,128)(2,1)}), bf16[128,64,1024]{2,1,0:T(8,128)(2,1)}) %all-gather.6.cloned.1.call-update) | async-done | bytes 16777232 | tf_op jit(solution)/shard_map/all_gather | solution.py:276
  176.5 2.0 broadcast_in_dim.133.grads_in
  191.4 6.2 %fusion.68 = bf16[4096,128]{1,0:T(8,128)(2,1)S(1)} fusion(s32[4096]{0:T(1024)S(1)} %broadcast_in_dim.151, s32[4096]{0:T(1024)S(1)} %broadcast_in_dim.142, s32[4096]{0:T(1024)S(1)} %broadcast_in_dim.139, s32[4096]{0:T(1024)S(1)} %rem.188, s32[4096]{0:T(1024)S(1)} %broadcast_add_fusion.1, s32[4096]{0:T(1024)S(1)} %broadcast_in_dim.115, ...), kind=kLoop, calls=%fused_computation.34.clone.clone.2 | loop fusion | flops 11534336 | bytes 1165568 | tf_op jit(solution)/shard_map/dot_general | solution.py:294
  197.5 33.8 %collective-permute-done.5.g_hbm = bf16[128,4096]{1,0:T(8,128)(2,1)S(1)} collective-permute-done((bf16[128,4096]{1,0:T(8,128)(2,1)S(1)}, bf16[128,4096]{1,0:T(8,128)(2,1)S(1)}, u32[]{:S(2)}, u32[]{:S(2)}) %collective-permute-start.5) | collective-permute-done | bytes 1048608 | tf_op jit(solution)/shard_map/ppermute | solution.py:310
  231.3 10.3 %chain_1_0.1 = (bf16[128,4096]{1,0:T(8,128)(2,1)S(1)}, bf16[384,4096]{1,0:T(8,128)(2,1)}, f32[384,128]{1,0:T(8,128)S(1)}, f32[384,128]{1,0:T(8,128)S(1)}) custom-call(s32[1]{0:T(128)} %bitcast.meta.refs_0_, bf16[128,4096]{1,0:T(8,128)(2,1)S(1)} %collective-permute-done.5.g_hbm, ...), custom_call_target="tpu_custom_call", output_to_operand_aliasing={{1}: (7, {}), {2}: (8, {}), {3}: (9, {})} | custom-call | flops 2147483648 | bytes 16777216 | tf_op jit(solution)/shard_map/chain_1_0/pallas_call | solution.py:147
  241.7 1.4 collective-permute-start.8
  243.0 2.8 collective-permute-done.4.g_hbm
  245.8 10.6 %chain_1_1.1 = (bf16[128,4096]{1,0:T(8,128)(2,1)S(1)}, bf16[384,4096]{1,0:T(8,128)(2,1)}, f32[384,128]{1,0:T(8,128)S(1)}, f32[384,128]{1,0:T(8,128)S(1)}) custom-call(s32[1]{0:T(128)} %bitcast.meta.refs_0_, bf16[128,4096]{1,0:T(8,128)(2,1)S(1)} %collective-permute-done.4.g_hbm, ...), custom_call_target="tpu_custom_call", output_to_operand_aliasing={{1}: (7, {}), {2}: (8, {}), {3}: (9, {})} | custom-call | flops 2147483648 | bytes 16777216 | tf_op jit(solution)/shard_map/chain_1_1/pallas_call | solution.py:147
  256.5 1.4 collective-permute-start.7
  257.9 22.4 %collective-permute-done.3.g_hbm = bf16[128,4096]{1,0:T(8,128)(2,1)S(1)} collective-permute-done((bf16[128,4096]{1,0:T(8,128)(2,1)S(1)}, bf16[128,4096]{1,0:T(8,128)(2,1)S(1)}, u32[]{:S(2)}, u32[]{:S(2)}) %collective-permute-start.3) | collective-permute-done | bytes 1048608 | tf_op jit(solution)/shard_map/ppermute | solution.py:310
  280.2 10.3 %chain_1_2.1 = (bf16[128,4096]{1,0:T(8,128)(2,1)S(1)}, bf16[384,4096]{1,0:T(8,128)(2,1)}, f32[384,128]{1,0:T(8,128)S(1)}, f32[384,128]{1,0:T(8,128)S(1)}) custom-call(s32[1]{0:T(128)} %bitcast.meta.refs_0_, bf16[128,4096]{1,0:T(8,128)(2,1)S(1)} %collective-permute-done.3.g_hbm, ...), custom_call_target="tpu_custom_call", output_to_operand_aliasing={{1}: (7, {}), {2}: (8, {}), {3}: (9, {})} | custom-call | flops 2147483648 | bytes 16777216 | tf_op jit(solution)/shard_map/chain_1_2/pallas_call | solution.py:147
  290.6 1.4 collective-permute-start.6
  291.9 1.7 fusion.4.hp
  293.6 6.3 %value_proj.1.vp = f32[384,128]{1,0:T(8,128)S(1)} custom-call(bf16[384,4096]{1,0:T(8,128)(2,1)S(1)} %fusion.2.h, bf16[64,2,64,1024]{3,2,1,0:T(8,128)(2,1)} %bitcast.57, bf16[1024,128]{1,0:T(8,128)(2,1)S(1)} %fusion.47.qm.refs_6_, bf16[128,4096]{1,0:T(8,128)(2,1)S(1)} %get-tuple-element.53.after), custom_call_target="tpu_custom_call" | custom-call | flops 3221225472 | bytes 8388608 | tf_op jit(solution)/shard_map/value_proj/pallas_call | solution.py:209
  304.6 2.2 copy-done.7
  308.6 4.9 %score.1 = f32[3,64]{1,0:T(4,128)S(1)} custom-call(s32[64]{0:T(128)S(1)} %copy-done.16, s32[3]{0:T(128)S(1)} %copy-done.15, f32[384,128]{1,0:T(8,128)S(1)} %copy-done.14, f32[384,128]{1,0:T(8,128)S(1)} %copy-done.13, f32[384,128]{1,0:T(8,128)S(1)} %copy-done.4, f32[384,128]{1,0:T(8,128)S(1)} %copy-done.6, bf16[64,256,128]{2,1,0:T(8,128)(2,1)S(1)} %copy-done.7), custom_call_target="tpu_custom_call" | custom-call | tf_op jit(solution)/shard_map/score/pallas_call | solution.py:260
  313.6 3.3 %collective-permute-start.11 = (f32[3,64]{1,0:T(4,128)S(1)}, f32[3,64]{1,0:T(4,128)S(1)}, u32[]{:S(2)}, u32[]{:S(2)}) collective-permute-start(f32[3,64]{1,0:T(4,128)S(1)} %score.1), channel_id=1, source_target_pairs={{0,192},{64,0},{128,64},{192,128},{1,193},{65,1},{129,65},{193,129... | collective-permute-start | bytes 2312 | tf_op jit(solution)/shard_map/ppermute | solution.py:318
  316.9 1.6 collective-permute-start.9
  318.5 1.6 collective-permute-done.11
  (123 shorter events, 32.4 us)
Async XLA Ops:
  7.2 169.3 %all-gather.6.cloned.1.call-start = ((), (), s32[]{:S(2)}) async-start(), calls=%async_computation.1 | async-start | bytes 17039360 | tf_op jit(solution)/shard_map/all_gather | solution.py:276
  8.9 293.8 %all-gather.4.cloned.1.call-start = ((), (), s32[]{:S(2)}) async-start(), calls=%async_computation | async-start | bytes 4259840 | tf_op jit(solution)/shard_map/all_gather | solution.py:287
  10.4 16.5 %copy-start.15 = (s32[3]{0:T(128)S(1)}, s32[3]{0:T(128)}, u32[]{:S(2)}) copy-start(s32[3]{0:T(128)} %lens.1) | copy-start | bytes 40
  18.7 16.6 %copy-start.17 = (bf16[384,4096]{1,0:T(8,128)(2,1)S(1)}, bf16[384,4096]{1,0:T(8,128)(2,1)}, u32[]{:S(2)}) copy-start(bf16[384,4096]{1,0:T(8,128)(2,1)} %param.11) | copy-start | bytes 9437188
  37.3 141.3 %copy-start = (bf16[1,384,4096]{2,1,0:T(8,128)(2,1)S(1)}, bf16[1,384,4096]{2,1,0:T(8,128)(2,1)}, u32[]{:S(2)}) copy-start(bf16[1,384,4096]{2,1,0:T(8,128)(2,1)} %param.10) | copy-start | bytes 9437188
  37.3 141.3 %copy-start.11 = (f32[1,4096]{1,0:T(1,128)S(1)}, f32[1,4096]{1,0:T(1,128)}, u32[]{:S(2)}) copy-start(f32[1,4096]{1,0:T(1,128)} %refs_3_.5) | copy-start | bytes 49156
  181.4 4.7 %collective-permute-start.2 = (bf16[128,4096]{1,0:T(8,128)(2,1)S(1)}, bf16[128,4096]{1,0:T(8,128)(2,1)S(1)}, u32[]{:S(2)}, u32[]{:S(2)}) collective-permute-start(bf16[128,4096]{1,0:T(8,128)(2,1)S(1)} %get-tuple-element.55), channel_id=1, source_target_pairs={{192,128},{193,129},{194,130},{195,131},{196,132},{197,133},{198,1... | collective-permute-start | bytes 3145736 | tf_op jit(solution)/shard_map/ppermute | solution.py:310
  182.9 4.8 %collective-permute-start.1 = (bf16[128,4096]{1,0:T(8,128)(2,1)S(1)}, bf16[128,4096]{1,0:T(8,128)(2,1)S(1)}, u32[]{:S(2)}, u32[]{:S(2)}) collective-permute-start(bf16[128,4096]{1,0:T(8,128)(2,1)S(1)} %get-tuple-element.54), channel_id=1, source_target_pairs={{192,128},{193,129},{194,130},{195,131},{196,132},{197,133},{198,1... | collective-permute-start | bytes 3145736 | tf_op jit(solution)/shard_map/ppermute | solution.py:310
  184.1 5.4 %collective-permute-start = (bf16[128,4096]{1,0:T(8,128)(2,1)S(1)}, bf16[128,4096]{1,0:T(8,128)(2,1)S(1)}, u32[]{:S(2)}, u32[]{:S(2)}) collective-permute-start(bf16[128,4096]{1,0:T(8,128)(2,1)S(1)} %get-tuple-element.53.after), channel_id=1, source_target_pairs={{192,128},{193,129},{194,130},{195,131},{196,132},{197,133},{198,1... | collective-permute-start | bytes 3145736 | tf_op jit(solution)/shard_map/ppermute | solution.py:310
  186.4 44.9 %collective-permute-start.5 = (bf16[128,4096]{1,0:T(8,128)(2,1)S(1)}, bf16[128,4096]{1,0:T(8,128)(2,1)S(1)}, u32[]{:S(2)}, u32[]{:S(2)}) collective-permute-start(bf16[128,4096]{1,0:T(8,128)(2,1)S(1)} %get-tuple-element.67), channel_id=1, source_target_pairs={{128,64},{129,65},{130,66},{131,67},{132,68},{133,69},{134,70},{13... | collective-permute-start | bytes 3145736 | tf_op jit(solution)/shard_map/ppermute | solution.py:310
  188.2 57.6 %collective-permute-start.4 = (bf16[128,4096]{1,0:T(8,128)(2,1)S(1)}, bf16[128,4096]{1,0:T(8,128)(2,1)S(1)}, u32[]{:S(2)}, u32[]{:S(2)}) collective-permute-start(bf16[128,4096]{1,0:T(8,128)(2,1)S(1)} %get-tuple-element.66), channel_id=1, source_target_pairs={{128,64},{129,65},{130,66},{131,67},{132,68},{133,69},{134,70},{13... | collective-permute-start | bytes 3145736 | tf_op jit(solution)/shard_map/ppermute | solution.py:310
  189.6 1.7 copy-start.18
  189.6 1.7 copy-start.19
  189.6 1.7 copy-start.21
  189.6 1.7 copy-start.22
  189.6 1.7 copy-start.23
  190.0 90.3 %collective-permute-start.3 = (bf16[128,4096]{1,0:T(8,128)(2,1)S(1)}, bf16[128,4096]{1,0:T(8,128)(2,1)S(1)}, u32[]{:S(2)}, u32[]{:S(2)}) collective-permute-start(bf16[128,4096]{1,0:T(8,128)(2,1)S(1)} %get-tuple-element.65), channel_id=1, source_target_pairs={{128,64},{129,65},{130,66},{131,67},{132,68},{133,69},{134,70},{13... | collective-permute-start | bytes 3145736 | tf_op jit(solution)/shard_map/ppermute | solution.py:310
  241.7 58.3 %collective-permute-start.8 = (bf16[128,4096]{1,0:T(8,128)(2,1)S(1)}, bf16[128,4096]{1,0:T(8,128)(2,1)S(1)}, u32[]{:S(2)}, u32[]{:S(2)}) collective-permute-start(bf16[128,4096]{1,0:T(8,128)(2,1)S(1)} %get-tuple-element.79), channel_id=1, source_target_pairs={{64,0},{65,1},{66,2},{67,3},{68,4},{69,5},{70,6},{71,7},{72,8},{73... | collective-permute-start | bytes 3145736 | tf_op jit(solution)/shard_map/ppermute | solution.py:310
  256.5 44.2 %collective-permute-start.7 = (bf16[128,4096]{1,0:T(8,128)(2,1)S(1)}, bf16[128,4096]{1,0:T(8,128)(2,1)S(1)}, u32[]{:S(2)}, u32[]{:S(2)}) collective-permute-start(bf16[128,4096]{1,0:T(8,128)(2,1)S(1)} %get-tuple-element.78), channel_id=1, source_target_pairs={{64,0},{65,1},{66,2},{67,3},{68,4},{69,5},{70,6},{71,7},{72,8},{73... | collective-permute-start | bytes 3145736 | tf_op jit(solution)/shard_map/ppermute | solution.py:310
  290.6 10.4 %collective-permute-start.6 = (bf16[128,4096]{1,0:T(8,128)(2,1)S(1)}, bf16[128,4096]{1,0:T(8,128)(2,1)S(1)}, u32[]{:S(2)}, u32[]{:S(2)}) collective-permute-start(bf16[128,4096]{1,0:T(8,128)(2,1)S(1)} %get-tuple-element.77), channel_id=1, source_target_pairs={{64,0},{65,1},{66,2},{67,3},{68,4},{69,5},{70,6},{71,7},{72,8},{73... | collective-permute-start | bytes 3145736 | tf_op jit(solution)/shard_map/ppermute | solution.py:310
  304.6 2.2 copy-start.7
  313.6 4.9 %collective-permute-start.10 = (f32[3,64]{1,0:T(4,128)S(1)}, f32[3,64]{1,0:T(4,128)S(1)}, u32[]{:S(2)}, u32[]{:S(2)}) collective-permute-start(f32[3,64]{1,0:T(4,128)S(1)} %score.1), channel_id=1, source_target_pairs={{0,128},{64,192},{128,0},{192,64},{1,129},{65,193},{129,1},{193,65... | collective-permute-start | bytes 2312 | tf_op jit(solution)/shard_map/ppermute | solution.py:318
  313.6 6.5 %collective-permute-start.11 = (f32[3,64]{1,0:T(4,128)S(1)}, f32[3,64]{1,0:T(4,128)S(1)}, u32[]{:S(2)}, u32[]{:S(2)}) collective-permute-start(f32[3,64]{1,0:T(4,128)S(1)} %score.1), channel_id=1, source_target_pairs={{0,192},{64,0},{128,64},{192,128},{1,193},{65,1},{129,65},{193,129... | collective-permute-start | bytes 2312 | tf_op jit(solution)/shard_map/ppermute | solution.py:318
  316.9 3.1 collective-permute-start.9
  (17 other events, 20.2 us)
Sparse Core Ops, SparseCore 0:
  11.9 164.5 all-gather.5
  179.8 92.7 all-gather.3
